TPU v7x, 32 devices: a whole 2x2x4 slice. The times are simulated.
32 devices in a mesh: dom: 16 (over z, y, core), col: 2 (over x).
Axes of the slice: x: 2, y: 2, z: 4, core: 2. Of those that a mesh axis runs over, the one named last changes fastest.
Arguments:
- wave: float32 [65536, 32], P(('dom', 'col')), may hold values from -6 to 6
- mass_scale: float32 [65536], P(('dom', 'col')), may hold values from 0.5 to 2
- potential: float32 [65536], P(('dom', 'col')), may hold values from -1 to 1
- stiffness: float32 [125, 125], replicated
- cell_scale: float32 [1024], P(('dom', 'col')), may hold values from 0.5 to 2
- cell_map: int32 [125, 1024], P(None, ('dom', 'col')), may hold values from 0 to 3071, as said below
- send_left: int32 [16384], P(('dom', 'col')), may hold values from 0 to 2047
- send_right: int32 [16384], P(('dom', 'col')), may hold values from 0 to 2047
- support_node: int32 [16384], P(('dom', 'col')), may hold values from 0 to 2047
- support_atom: int32 [16384], P(('dom', 'col')), may hold values from 0 to 20, as said below
- projector: float32 [8, 16384], P(None, ('dom', 'col')), may hold values from -1 to 1
- coupling: float32 [8, 320], P(None, 'dom'), may hold values from 0.25 to 1.5
Outputs:
- filtered: float32 [65536, 32], P(('dom', 'col'))
Inputs may be any that keep to these rules, and one draw needn't show every extreme that they name: `cell_map`: local node numbers of the cell's partition: below 2048 an owned node, 2048 + i the i-th row received from the previous partition, 2560 + i the i-th row from the next one. The cells of a partition with local number below 24 name owned nodes only. `send_left`: local owned node numbers. `send_right`: local owned node numbers. `support_node`: local owned node numbers. `support_atom`: atom number within the neighbourhood; 20 marks an empty slot. A partition's empty slots follow its live ones, and some partition has none.
All inputs are finite; a program needn't handle non-finite values.
Results may differ from a plain program's by a relative error of at most 0.0003.
Values sent between devices are 32-bit elements; how exact they have to be, the bound alone decides.
A program may use at most 64 MiB of HBM per device.

v0:
```python
import jax
import jax.numpy as jnp
from jax import lax
from jax.sharding import PartitionSpec as P


def padded(block, sides, width):
    for axis, dim in sides:
        count = lax.axis_size(axis)
        forward = [(i, i + 1) for i in range(count - 1)]
        backward = [(target, source) for source, target in forward]
        low = lax.ppermute(
            lax.slice_in_dim(block, block.shape[dim] - width, None, axis=dim), axis, forward
        )
        high = lax.ppermute(lax.slice_in_dim(block, 0, width, axis=dim), axis, backward)
        block = jnp.concatenate([low, block, high], axis=dim)
    return block


def cell_terms(field, local_map, local_scale, stiffness, total_rows):
    gathered = field[local_map]
    product = jnp.dot(
        stiffness,
        gathered.reshape(gathered.shape[0], -1),
        precision=lax.Precision.HIGHEST,
        preferred_element_type=jnp.float32,
    )
    product = product.reshape(gathered.shape) * local_scale[None, :, None]
    return jnp.zeros((total_rows, gathered.shape[2]), jnp.float32).at[local_map].add(product)


def body(
    wave,
    mass_scale,
    potential,
    stiffness,
    cell_scale,
    cell_map,
    send_left,
    send_right,
    support_node,
    support_atom,
    projector,
    coupling,
):
    node_count = wave.shape[0]
    ghost_count = send_left.shape[0]
    total_rows = node_count + 2 * ghost_count
    atom_count = coupling.shape[1]
    highest = lax.Precision.HIGHEST
    atom_onehot = (
        support_atom[:, None] == jnp.arange(atom_count, dtype=jnp.int32)[None, :]
    ).astype(jnp.float32)

    def apply_ham(field):
        scaled = mass_scale[:, None] * field
        outgoing = jnp.concatenate([scaled[send_left], scaled[send_right]], axis=0)
        received = padded(outgoing, ((("dom", "col"), 0),), ghost_count)
        extended = jnp.concatenate(
            [scaled, received[:ghost_count], received[3 * ghost_count :]], axis=0
        )
        assembled = cell_terms(extended, cell_map, cell_scale, stiffness, total_rows)
        returning = jnp.concatenate(
            [
                assembled[node_count : node_count + ghost_count],
                assembled[node_count + ghost_count :],
            ],
            axis=0,
        )
        came_back = padded(returning, ((("dom", "col"), 0),), ghost_count)
        folded = assembled[:node_count]
        folded = folded.at[send_left].add(came_back[:ghost_count])
        folded = folded.at[send_right].add(came_back[3 * ghost_count :])
        partial_proj = jnp.einsum(
            "ea,je,ek->ajk", atom_onehot, projector, scaled[support_node], precision=highest
        )
        summed = lax.psum(partial_proj, "col")
        coefficients = summed * coupling.T[:, :, None]
        spread_back = jnp.einsum(
            "ea,je,ajk->ek", atom_onehot, projector, coefficients, precision=highest
        )
        folded = folded.at[support_node].add(spread_back)
        return mass_scale[:, None] * folded + potential[:, None] * field

    first = (apply_ham(wave) - 2.0 * wave) / 4.0
    return 2.0 * (apply_ham(first) - 2.0 * first) / 4.0 - wave


def solution(mesh):
    return jax.shard_map(
        body,
        mesh=mesh,
        in_specs=(
            P(("dom", "col"), None),
            P(("dom", "col")),
            P(("dom", "col")),
            P(),
            P(("dom", "col")),
            P(None, ("dom", "col")),
            P(("dom", "col")),
            P(("dom", "col")),
            P(("dom", "col")),
            P(("dom", "col")),
            P(None, ("dom", "col")),
            P(None, "dom"),
        ),
        out_specs=P(("dom", "col"), None),
        check_vma=False,
    )
```

profile of v0, /device:TPU:1, one launch (start us, length us, event | category | flops | bytes accessed | tf_op | source)
XLA Modules:
  0.0 189.1 jit_solution(350413395065112056)
XLA Ops:
  0.0 0.7 compare_select_fusion.2
  0.7 0.6 copy-done.8
  1.3 1.0 broadcast_multiply_fusion.2
  2.6 1.0 gather_fusion.1
  3.9 4.5 %collective-permute-start.1 = (f32[512,32]{0,1:T(8,128)S(1)}, f32[512,32]{0,1:T(8,128)S(1)}, u32[]{:S(2)}, u32[]{:S(2)}) collective-permute-start(f32[512,32]{0,1:T(8,128)S(1)} %copy.66), channel_id=1, source_target_pairs={{1,0},{2,1},{3,2},{4,3},{5,4},{6,5},{7,6},{8,7},{9,8},{10,9},{11,1... | collective-permute-start | bytes 196616 | tf_op jit(solution)/shard_map/ppermute | solution.py:15
  8.4 0.6 copy-done.10
  9.0 0.6 copy-done.20
  9.6 1.0 gather_fusion
  10.7 1.9 %collective-permute-start = (f32[512,32]{0,1:T(8,128)S(1)}, f32[512,32]{0,1:T(8,128)S(1)}, u32[]{:S(2)}, u32[]{:S(2)}) collective-permute-start(f32[512,32]{0,1:T(8,128)S(1)} %copy.64), channel_id=1, source_target_pairs={{0,1},{1,2},{2,3},{3,4},{4,5},{5,6},{6,7},{7,8},{8,9},{9,10},{10,1... | collective-permute-start | bytes 196616 | tf_op jit(solution)/shard_map/ppermute | solution.py:12
  12.7 0.6 broadcast_multiply_fusion.4
  13.3 0.6 broadcast_multiply_fusion.3
  14.1 1.0 gather_fusion.3
  15.2 0.5 convolution_bitcast_fusion.3
  15.7 8.5 %psum.14 = f32[20,8,32]{2,0,1:T(8,128)S(1)} all-reduce(f32[20,8,32]{2,0,1:T(8,128)S(1)} %convolution_bitcast_fusion.3), channel_id=1, replica_groups=mesh['dom'=16,'col'=2] {'col'}, use_global_device_ids=true, to_apply=%region_3.0 | all-reduce | flops 5120 | bytes 40960 | tf_op jit(solution)/shard_map/psum | solution.py:77
  24.8 14.1 %gather_fusion.2 = f32[4000,32]{1,0:T(8,128)} fusion(f32[3072,32]{1,0:T(8,128)S(1)} %copy.67, s32[4096]{0:T(1024)S(1)} %pad_clamp_fusion), kind=kCustom, calls=%fused_computation.2 | custom fusion | bytes 1040000 | tf_op jit(solution)/shard_map/gather | solution.py:21
  38.8 2.4 %reshape.17 = f32[125,1024]{1,0:T(8,128)S(1)} reshape(f32[4000,32]{1,0:T(8,128)} %gather_fusion.2) | data formatting | bytes 1024000 | tf_op jit(solution)/shard_map/reshape | solution.py:24
  41.3 1.0 fusion.30
  42.4 2.8 %copy.68 = f32[125,32,32]{2,1,0:T(8,128)} copy(f32[125,32,32]{0,2,1:T(8,128)S(1)} %broadcast_multiply_fusion.1) | data formatting | bytes 1024000 | tf_op jit(solution)/shard_map/mul | solution.py:28
  45.3 23.1 %scatter_custom_fusion = f32[3072,32]{1,0:T(8,128)S(1)} fusion(s32[4000]{0:T(1024)S(1)} %reshape.119, f32[4000,32]{1,0:T(8,128)} %bitcast.40, f32[]{:T(128)} %constant.4.clone.1), kind=kCustom, calls=%fused_computation.22 | custom fusion | flops 128000 | bytes 393728 | tf_op jit(solution)/shard_map/scatter-add | solution.py:29
  68.4 0.7 fusion.29
  69.1 3.3 %collective-permute-start.3 = (f32[512,32]{1,0:T(8,128)}, f32[512,32]{1,0:T(8,128)S(1)}, u32[]{:S(2)}, u32[]{:S(2)}) collective-permute-start(f32[512,32]{1,0:T(8,128)} %get-tuple-element.7), channel_id=1, source_target_pairs={{1,0},{2,1},{3,2},{4,3},{5,4},{6,5},{7,6},{8,7},{9,8},{10,9},{11,1... | collective-permute-start | bytes 196616 | tf_op jit(solution)/shard_map/ppermute | solution.py:15
  72.4 2.0 %collective-permute-start.2 = (f32[512,32]{1,0:T(8,128)S(1)}, f32[512,32]{1,0:T(8,128)S(1)}, u32[]{:S(2)}, u32[]{:S(2)}) collective-permute-start(f32[512,32]{1,0:T(8,128)S(1)} %get-tuple-element.8), channel_id=1, source_target_pairs={{0,1},{1,2},{2,3},{3,4},{4,5},{5,6},{6,7},{7,8},{8,9},{9,10},{10,1... | collective-permute-start | bytes 196616 | tf_op jit(solution)/shard_map/ppermute | solution.py:12
  74.4 1.1 convolution_bitcast_fusion.1
  75.6 9.3 %collective-permute-done.2 = f32[512,32]{1,0:T(8,128)S(1)} collective-permute-done((f32[512,32]{1,0:T(8,128)S(1)}, f32[512,32]{1,0:T(8,128)S(1)}, u32[]{:S(2)}, u32[]{:S(2)}) %collective-permute-start.2) | collective-permute-done | bytes 65568 | tf_op jit(solution)/shard_map/ppermute | solution.py:12
  84.9 4.0 %scatter_fusion = f32[2048,32]{1,0:T(8,128)S(1)} fusion(f32[2048,32]{1,0:T(8,128)S(1)} %slice.40, s32[512]{0:T(512)} %copy-done.8, f32[512,32]{1,0:T(8,128)S(1)} %collective-permute-done.2), kind=kCustom, calls=%fused_computation.9 | custom fusion | flops 16384 | bytes 198656 | tf_op jit(solution)/shard_map/scatter-add | solution.py:72
  88.9 3.7 %scatter_fusion.1 = f32[2048,32]{1,0:T(8,128)S(1)} fusion(f32[2048,32]{1,0:T(8,128)S(1)} %scatter_fusion, s32[512]{0:T(512)S(1)} %copy-done.11, f32[512,32]{1,0:T(8,128)S(1)} %collective-permute-done.3), kind=kCustom, calls=%fused_computation.10 | custom fusion | flops 16384 | bytes 198656 | tf_op jit(solution)/shard_map/scatter-add | solution.py:73
  92.6 3.7 %scatter_fusion.2 = f32[2048,32]{1,0:T(8,128)S(1)} fusion(f32[2048,32]{1,0:T(8,128)S(1)} %scatter_fusion.1, s32[512]{0:T(512)S(1)} %copy-done.14, f32[512,32]{1,0:T(8,128)S(1)} %convolution_bitcast_fusion.1), kind=kCustom, calls=%fused_computation.11 | custom fusion | flops 16384 | bytes 198656 | tf_op jit(solution)/shard_map/scatter-add | solution.py:82
  97.1 1.0 gather_fusion.7
  98.1 1.0 gather_fusion.5
  99.2 1.0 gather_fusion.4
  100.4 3.1 %collective-permute-start.5 = (f32[512,32]{0,1:T(8,128)S(1)}, f32[512,32]{0,1:T(8,128)S(1)}, u32[]{:S(2)}, u32[]{:S(2)}) collective-permute-start(f32[512,32]{0,1:T(8,128)S(1)} %copy.76), channel_id=1, source_target_pairs={{1,0},{2,1},{3,2},{4,3},{5,4},{6,5},{7,6},{8,7},{9,8},{10,9},{11,1... | collective-permute-start | bytes 196616 | tf_op jit(solution)/shard_map/ppermute | solution.py:15
  103.5 2.2 %collective-permute-start.4 = (f32[512,32]{0,1:T(8,128)S(1)}, f32[512,32]{0,1:T(8,128)S(1)}, u32[]{:S(2)}, u32[]{:S(2)}) collective-permute-start(f32[512,32]{0,1:T(8,128)S(1)} %copy.74), channel_id=1, source_target_pairs={{0,1},{1,2},{2,3},{3,4},{4,5},{5,6},{6,7},{7,8},{8,9},{9,10},{10,1... | collective-permute-start | bytes 196616 | tf_op jit(solution)/shard_map/ppermute | solution.py:12
  105.8 0.5 convolution_bitcast_fusion.2
  106.2 9.2 %psum.15 = f32[20,8,32]{2,0,1:T(8,128)S(1)} all-reduce(f32[20,8,32]{2,0,1:T(8,128)S(1)} %convolution_bitcast_fusion.2), channel_id=1, replica_groups=mesh['dom'=16,'col'=2] {'col'}, use_global_device_ids=true, to_apply=%region_8.0 | all-reduce | flops 5120 | bytes 40960 | tf_op jit(solution)/shard_map/psum | solution.py:77
  116.0 14.1 %gather_fusion.6 = f32[4000,32]{1,0:T(8,128)} fusion(f32[3072,32]{1,0:T(8,128)S(1)} %copy.77, s32[4096]{0:T(1024)S(1)} %pad_clamp_fusion), kind=kCustom, calls=%fused_computation.6 | custom fusion | bytes 1040000 | tf_op jit(solution)/shard_map/gather | solution.py:21
  130.1 2.4 %reshape.19 = f32[125,1024]{1,0:T(8,128)S(1)} reshape(f32[4000,32]{1,0:T(8,128)} %gather_fusion.6) | data formatting | bytes 1024000 | tf_op jit(solution)/shard_map/reshape | solution.py:24
  132.5 1.0 fusion.31
  133.7 2.8 %copy.78 = f32[125,32,32]{2,1,0:T(8,128)} copy(f32[125,32,32]{0,2,1:T(8,128)S(1)} %broadcast_multiply_fusion) | data formatting | bytes 1024000 | tf_op jit(solution)/shard_map/mul | solution.py:28
  136.5 23.1 %scatter_custom_fusion.4 = f32[3072,32]{1,0:T(8,128)S(1)} fusion(s32[4000]{0:T(1024)} %copy-done.5, f32[4000,32]{1,0:T(8,128)} %bitcast.39, f32[]{:T(128)} %constant.4.clone.1), kind=kCustom, calls=%fused_computation.20 | custom fusion | flops 128000 | bytes 393728 | tf_op jit(solution)/shard_map/scatter-add | solution.py:29
  159.6 0.7 fusion.28
  160.3 2.5 %collective-permute-start.7 = (f32[512,32]{1,0:T(8,128)}, f32[512,32]{1,0:T(8,128)S(1)}, u32[]{:S(2)}, u32[]{:S(2)}) collective-permute-start(f32[512,32]{1,0:T(8,128)} %get-tuple-element.5), channel_id=1, source_target_pairs={{1,0},{2,1},{3,2},{4,3},{5,4},{6,5},{7,6},{8,7},{9,8},{10,9},{11,1... | collective-permute-start | bytes 196616 | tf_op jit(solution)/shard_map/ppermute | solution.py:15
  162.8 2.8 %collective-permute-start.6 = (f32[512,32]{1,0:T(8,128)S(1)}, f32[512,32]{1,0:T(8,128)}, u32[]{:S(2)}, u32[]{:S(2)}) collective-permute-start(f32[512,32]{1,0:T(8,128)S(1)} %get-tuple-element.6), channel_id=1, source_target_pairs={{0,1},{1,2},{2,3},{3,4},{4,5},{5,6},{6,7},{7,8},{8,9},{9,10},{10,1... | collective-permute-start | bytes 196616 | tf_op jit(solution)/shard_map/ppermute | solution.py:12
  165.6 1.8 convolution_bitcast_fusion
  167.5 8.7 %collective-permute-done.6 = f32[512,32]{1,0:T(8,128)} collective-permute-done((f32[512,32]{1,0:T(8,128)S(1)}, f32[512,32]{1,0:T(8,128)}, u32[]{:S(2)}, u32[]{:S(2)}) %collective-permute-start.6) | collective-permute-done | bytes 65568 | tf_op jit(solution)/shard_map/ppermute | solution.py:12
  176.2 4.1 %scatter_fusion.3 = f32[2048,32]{1,0:T(8,128)S(1)} fusion(f32[2048,32]{1,0:T(8,128)S(1)} %slice.43, s32[512]{0:T(512)S(1)} %copy-done.9, f32[512,32]{1,0:T(8,128)} %collective-permute-done.6), kind=kCustom, calls=%fused_computation.13 | custom fusion | flops 16384 | bytes 198656 | tf_op jit(solution)/shard_map/scatter-add | solution.py:72
  180.3 4.0 %scatter_fusion.4 = f32[2048,32]{1,0:T(8,128)S(1)} fusion(f32[2048,32]{1,0:T(8,128)S(1)} %scatter_fusion.3, s32[512]{0:T(512)S(1)} %copy-done.12, f32[512,32]{1,0:T(8,128)S(1)} %collective-permute-done.7), kind=kCustom, calls=%fused_computation.14 | custom fusion | flops 16384 | bytes 198656 | tf_op jit(solution)/shard_map/scatter-add | solution.py:73
  184.3 3.7 %scatter_fusion.5 = f32[2048,32]{1,0:T(8,128)S(1)} fusion(f32[2048,32]{1,0:T(8,128)S(1)} %scatter_fusion.4, s32[512]{0:T(512)S(1)} %copy-done.14, f32[512,32]{1,0:T(8,128)S(1)} %copy-done.2), kind=kCustom, calls=%fused_computation.15 | custom fusion | flops 16384 | bytes 198656 | tf_op jit(solution)/shard_map/scatter-add | solution.py:82
  188.3 0.8 multiply_subtract_fusion
  (92 shorter events, 3.5 us)
Async XLA Ops:
  0.0 41.3 %copy-start = (f32[125,125]{1,0:T(8,128)S(1)}, f32[125,125]{1,0:T(8,128)}, u32[]{:S(2)}) copy-start(f32[125,125]{1,0:T(8,128)} %param.15) | copy-start | bytes 187504
  0.7 0.6 copy-start.8
  1.3 1.3 copy-start.18
  2.3 6.1 %copy-start.27 = (s32[512]{0:T(512)S(1)}, s32[512]{0:T(512)}, u32[]{:S(2)}) copy-start(s32[512]{0:T(512)} %param.19) | copy-start | bytes 6148
  3.7 9.0 %copy-start.3 = (f32[2048]{0:T(1024)S(1)}, f32[2048]{0:T(1024)}, u32[]{:S(2)}) copy-start(f32[2048]{0:T(1024)} %param.13) | copy-start | bytes 24580
  3.7 9.6 %copy-start.28 = (s32[512]{0:T(512)S(1)}, s32[512]{0:T(512)}, u32[]{:S(2)}) copy-start(s32[512]{0:T(512)} %param.20) | copy-start | bytes 6148
  3.7 9.6 %copy-start.4 = (f32[2048]{0:T(1024)S(1)}, f32[2048]{0:T(1024)}, u32[]{:S(2)}) copy-start(f32[2048]{0:T(1024)} %param.14) | copy-start | bytes 24580
  3.7 10.2 %copy-start.17 = (s32[125,32]{0,1:T(8,128)S(1)}, s32[125,32]{0,1:T(8,128)}, u32[]{:S(2)}) copy-start(s32[125,32]{0,1:T(8,128)} %param.17) | copy-start | bytes 48004
  3.7 10.2 %copy-start.26 = (s32[512]{0:T(512)S(1)}, s32[512]{0:T(512)}, u32[]{:S(2)}) copy-start(s32[512]{0:T(512)} %param.21) | copy-start | bytes 6148
  3.9 20.4 %collective-permute-start.1 = (f32[512,32]{0,1:T(8,128)S(1)}, f32[512,32]{0,1:T(8,128)S(1)}, u32[]{:S(2)}, u32[]{:S(2)}) collective-permute-start(f32[512,32]{0,1:T(8,128)S(1)} %copy.66), channel_id=1, source_target_pairs={{1,0},{2,1},{3,2},{4,3},{5,4},{6,5},{7,6},{8,7},{9,8},{10,9},{11,1... | collective-permute-start | bytes 196616 | tf_op jit(solution)/shard_map/ppermute | solution.py:15
  8.4 0.6 copy-start.10
  9.0 0.6 copy-start.20
  10.6 4.6 %copy-start.6 = (f32[8,512]{1,0:T(8,128)S(1)}, f32[8,512]{1,0:T(8,128)}, u32[]{:S(2)}) copy-start(f32[8,512]{1,0:T(8,128)} %param.22) | copy-start | bytes 49156
  10.7 13.5 %collective-permute-start = (f32[512,32]{0,1:T(8,128)S(1)}, f32[512,32]{0,1:T(8,128)S(1)}, u32[]{:S(2)}, u32[]{:S(2)}) collective-permute-start(f32[512,32]{0,1:T(8,128)S(1)} %copy.64), channel_id=1, source_target_pairs={{0,1},{1,2},{2,3},{3,4},{4,5},{5,6},{6,7},{7,8},{8,9},{9,10},{10,1... | collective-permute-start | bytes 196616 | tf_op jit(solution)/shard_map/ppermute | solution.py:12
  13.3 0.7 copy-start.13
  13.3 11.0 %copy-start.22 = (s32[1024]{0:T(1024)}, s32[1024]{0:T(1024)S(1)}, u32[]{:S(2)}) copy-start(s32[1024]{0:T(1024)S(1)} %pad_clamp_fusion.1) | copy-start | bytes 12292
  14.1 31.1 %copy-start.5 = (s32[4000]{0:T(1024)}, s32[4000]{0:T(1024)S(1)}, u32[]{:S(2)}) copy-start(s32[4000]{0:T(1024)S(1)} %reshape.119) | copy-start | bytes 48004
  38.8 3.5 %copy-start.24 = (f32[32]{0:T(128)S(1)}, f32[32]{0:T(128)}, u32[]{:S(2)}) copy-start(f32[32]{0:T(128)} %param.16) | copy-start | bytes 388
  42.4 32.0 %copy-start.29 = (f32[8,20]{1,0:T(8,128)S(1)}, f32[8,20]{1,0:T(8,128)}, u32[]{:S(2)}) copy-start(f32[8,20]{1,0:T(8,128)} %param.23) | copy-start | bytes 1924
  69.1 19.7 %collective-permute-start.3 = (f32[512,32]{1,0:T(8,128)}, f32[512,32]{1,0:T(8,128)S(1)}, u32[]{:S(2)}, u32[]{:S(2)}) collective-permute-start(f32[512,32]{1,0:T(8,128)} %get-tuple-element.7), channel_id=1, source_target_pairs={{1,0},{2,1},{3,2},{4,3},{5,4},{6,5},{7,6},{8,7},{9,8},{10,9},{11,1... | collective-permute-start | bytes 196616 | tf_op jit(solution)/shard_map/ppermute | solution.py:15
  72.4 12.4 %collective-permute-start.2 = (f32[512,32]{1,0:T(8,128)S(1)}, f32[512,32]{1,0:T(8,128)S(1)}, u32[]{:S(2)}, u32[]{:S(2)}) collective-permute-start(f32[512,32]{1,0:T(8,128)S(1)} %get-tuple-element.8), channel_id=1, source_target_pairs={{0,1},{1,2},{2,3},{3,4},{4,5},{5,6},{6,7},{7,8},{8,9},{9,10},{10,1... | collective-permute-start | bytes 196616 | tf_op jit(solution)/shard_map/ppermute | solution.py:12
  75.6 13.3 %copy-start.11 = (s32[512]{0:T(512)S(1)}, s32[512]{0:T(512)}, u32[]{:S(2)}) copy-start(s32[512]{0:T(512)} %copy-done.10) | copy-start | bytes 6148
  88.8 3.7 %copy-start.14 = (s32[512]{0:T(512)S(1)}, s32[512]{0:T(512)}, u32[]{:S(2)}) copy-start(s32[512]{0:T(512)} %copy-done.13) | copy-start | bytes 6148
  92.6 4.0 %copy-start.1 = (f32[2048,32]{0,1:T(8,128)S(1)}, f32[2048,32]{0,1:T(8,128)}, u32[]{:S(2)}) copy-start(f32[2048,32]{0,1:T(8,128)} %param.12) | copy-start | bytes 786436
  92.6 4.0 %copy-start.16 = (f32[2048]{0:T(1024)S(1)}, f32[2048]{0:T(1024)}, u32[]{:S(2)}) copy-start(f32[2048]{0:T(1024)} %broadcast_multiply_fusion.4) | copy-start | bytes 24580
  96.3 0.7 copy-start.23
  96.6 1.5 copy-start.19
  97.1 2.1 %copy-start.21 = (s32[1024]{0:T(1024)S(1)}, s32[1024]{0:T(1024)}, u32[]{:S(2)}) copy-start(s32[1024]{0:T(1024)} %copy-done.20) | copy-start | bytes 12292
  99.2 6.6 %copy-start.7 = (f32[8,512]{1,0:T(8,128)S(1)}, f32[8,512]{1,0:T(8,128)}, u32[]{:S(2)}) copy-start(f32[8,512]{1,0:T(8,128)} %param.22) | copy-start | bytes 49156
  100.4 15.0 %collective-permute-start.5 = (f32[512,32]{0,1:T(8,128)S(1)}, f32[512,32]{0,1:T(8,128)S(1)}, u32[]{:S(2)}, u32[]{:S(2)}) collective-permute-start(f32[512,32]{0,1:T(8,128)S(1)} %copy.76), channel_id=1, source_target_pairs={{1,0},{2,1},{3,2},{4,3},{5,4},{6,5},{7,6},{8,7},{9,8},{10,9},{11,1... | collective-permute-start | bytes 196616 | tf_op jit(solution)/shard_map/ppermute | solution.py:15
  103.5 12.0 %collective-permute-start.4 = (f32[512,32]{0,1:T(8,128)S(1)}, f32[512,32]{0,1:T(8,128)S(1)}, u32[]{:S(2)}, u32[]{:S(2)}) collective-permute-start(f32[512,32]{0,1:T(8,128)S(1)} %copy.74), channel_id=1, source_target_pairs={{0,1},{1,2},{2,3},{3,4},{4,5},{5,6},{6,7},{7,8},{8,9},{9,10},{10,1... | collective-permute-start | bytes 196616 | tf_op jit(solution)/shard_map/ppermute | solution.py:12
  130.1 3.5 %copy-start.25 = (f32[32]{0:T(128)S(1)}, f32[32]{0:T(128)}, u32[]{:S(2)}) copy-start(f32[32]{0:T(128)} %param.16) | copy-start | bytes 388
  133.7 32.0 %copy-start.30 = (f32[8,20]{1,0:T(8,128)S(1)}, f32[8,20]{1,0:T(8,128)}, u32[]{:S(2)}) copy-start(f32[8,20]{1,0:T(8,128)} %param.23) | copy-start | bytes 1924
  159.6 16.6 %copy-start.9 = (s32[512]{0:T(512)S(1)}, s32[512]{0:T(512)}, u32[]{:S(2)}) copy-start(s32[512]{0:T(512)} %copy-done.8) | copy-start | bytes 6148
  160.3 19.9 %collective-permute-start.7 = (f32[512,32]{1,0:T(8,128)}, f32[512,32]{1,0:T(8,128)S(1)}, u32[]{:S(2)}, u32[]{:S(2)}) collective-permute-start(f32[512,32]{1,0:T(8,128)} %get-tuple-element.5), channel_id=1, source_target_pairs={{1,0},{2,1},{3,2},{4,3},{5,4},{6,5},{7,6},{8,7},{9,8},{10,9},{11,1... | collective-permute-start | bytes 196616 | tf_op jit(solution)/shard_map/ppermute | solution.py:15
  162.8 13.3 %collective-permute-start.6 = (f32[512,32]{1,0:T(8,128)S(1)}, f32[512,32]{1,0:T(8,128)}, u32[]{:S(2)}, u32[]{:S(2)}) collective-permute-start(f32[512,32]{1,0:T(8,128)S(1)} %get-tuple-element.6), channel_id=1, source_target_pairs={{0,1},{1,2},{2,3},{3,4},{4,5},{5,6},{6,7},{7,8},{8,9},{9,10},{10,1... | collective-permute-start | bytes 196616 | tf_op jit(solution)/shard_map/ppermute | solution.py:12
  167.5 12.8 %copy-start.12 = (s32[512]{0:T(512)S(1)}, s32[512]{0:T(512)}, u32[]{:S(2)}) copy-start(s32[512]{0:T(512)} %copy-done.10) | copy-start | bytes 6148
  180.3 4.0 %copy-start.2 = (f32[512,32]{1,0:T(8,128)S(1)}, f32[512,32]{1,0:T(8,128)}, u32[]{:S(2)}) copy-start(f32[512,32]{1,0:T(8,128)} %convolution_bitcast_fusion) | copy-start | bytes 196612
  184.3 4.0 %copy-start.15 = (f32[2048]{0:T(1024)S(1)}, f32[2048]{0:T(1024)}, u32[]{:S(2)}) copy-start(f32[2048]{0:T(1024)} %broadcast_multiply_fusion.3) | copy-start | bytes 24580
where the time goes:
time: 190 us; the launch traced here: 189 us
  other arithmetic  73.3 us (39%)
  local copies, waits for them, and re-layouts  51.2 us (27%)
  starting transfers between devices  22.2 us (12%)
  waiting for transfers between devices  17.9 us (9%)
  blocking collectives  17.8 us (9%)
  matrix products  5.84 us (3%)
    scatter-add x2, other arithmetic, cell_terms(): jnp.zeros((total_rows, gathered.shape[2]), jnp.float32).at[local_map]  46.2 us
    gather x2, local copies, waits for them, and re-layouts, cell_terms(): gathered = field[local_map]  28.2 us
    ppermute x4, waiting for transfers between devices, padded(): lax.ppermute(lax.slice_in_dim(block, block.shape[dim] - width, None, axis...  17.9 us
    psum x2, blocking collectives, apply_ham(): summed = lax.psum(partial_proj, 'col')  17.8 us
    ppermute x4, starting transfers between devices, padded(): lax.ppermute(lax.slice_in_dim(block, 0, width, axis=dim), axis, backward)  13.4 us
    ppermute x4, starting transfers between devices, padded(): lax.ppermute(lax.slice_in_dim(block, block.shape[dim] - width, None, axis...  8.85 us
    scatter-add x2, other arithmetic, apply_ham(): folded = folded.at[send_left].add(came_back[:ghost_count])  8.06 us
    scatter-add x2, other arithmetic, apply_ham(): folded = folded.at[send_right].add(came_back[3 * ghost_count:])  7.64 us
  transfers between devices with their start and end apart: 8, of which 2 were waited for; matrix products, arithmetic and copies ran while one was open for 8% of the time, Pallas kernels for 0%

commit v1 on v0

v1 whole, which is shorter than its diff:
```python
import functools

import jax
import jax.numpy as jnp
from jax import lax
from jax.experimental import pallas as pl
from jax.experimental.pallas import tpu as pltpu
from jax.sharding import PartitionSpec as P

L = 128
BF = jnp.bfloat16
F32 = jnp.float32
MESH = pl.DeviceIdType.MESH


def split(x):
    hi = x.astype(BF)
    return hi, (x - hi.astype(F32)).astype(BF)


def dot(a, b):
    return jnp.dot(a, b, preferred_element_type=F32)


def kernel(
    cfg,
    wave_ref, mass_ref, pot_ref, stiff_ref, scale_ref, map_ref,
    left_ref, right_ref, node_ref, atom_ref, proj_ref, coup_ref,
    out_ref,
    field, vcur, vwave, mass, pot, smat, cellrow,
    ohi, ohb, ohs, otm, otg, mask, z, acc,
    paf, pa, pat, cpl, coef,
    halo_send, halo_recv, back_send, back_recv, proj_send, proj_recv,
    hs_sem, hr_sem, bs_sem, br_sem, ps_sem, pr_sem,
):
    n_dom, n_col = cfg["n_dom"], cfg["n_col"]
    cols, groups, rows = cfg["cols"], cfg["groups"], cfg["rows"]
    cells, inner, width = cfg["cells"], cfg["inner"], cfg["cell_nodes"]
    nodes, ghost, slots = cfg["nodes"], cfg["ghost"], cfg["slots"]
    atoms, nproj = cfg["atoms"], cfg["nproj"]
    grows = ghost // groups
    tiles = rows // L
    sup0 = cells * L
    fold0 = sup0 + slots
    total = fold0 + 2 * ghost
    arows = atoms * nproj
    apad = paf.shape[0]

    dom = lax.axis_index("dom")
    col = lax.axis_index("col")
    me = dom * n_col + col
    last = n_dom * n_col - 1
    has_prev = me > 0
    has_next = me < last
    prev = jnp.maximum(me - 1, 0)
    after = jnp.minimum(me + 1, last)
    prev_id = (prev // n_col, prev % n_col)
    next_id = (after // n_col, after % n_col)
    outer_prev = jnp.logical_and(has_prev, col == 0)
    outer_next = jnp.logical_and(has_next, col == n_col - 1)

    zero_block = jnp.zeros((grows, L), F32)
    for it in range(2):
        @pl.when(jnp.logical_not(has_prev))
        def _():
            halo_recv[it, 0] = zero_block
            back_recv[it, 0] = zero_block

        @pl.when(jnp.logical_not(has_next))
        def _():
            halo_recv[it, 1] = zero_block
            back_recv[it, 1] = zero_block

    barrier = pltpu.get_barrier_semaphore()
    for k in range(1, n_col):
        pl.semaphore_signal(
            barrier, inc=1, device_id=(dom, (col + k) % n_col), device_id_type=MESH
        )

    @pl.when(outer_prev)
    def _():
        pl.semaphore_signal(barrier, inc=1, device_id=prev_id, device_id_type=MESH)

    @pl.when(outer_next)
    def _():
        pl.semaphore_signal(barrier, inc=1, device_id=next_id, device_id_type=MESH)

    lane = lax.broadcasted_iota(jnp.int32, (L, L), 1)
    sub = lax.broadcasted_iota(jnp.int32, (L, L), 0)
    lane_group = lane // cols

    def replicate(x):
        shift = L // 2
        while shift >= cols:
            x = x + pltpu.roll(x, shift, 1)
            shift //= 2
        return x

    for t in range(tiles):
        block = jnp.concatenate(
            [wave_ref[:, q * rows + t * L : q * rows + (t + 1) * L] for q in range(groups)], axis=0
        )
        block = block.T
        vcur[t * L : (t + 1) * L, :] = block
        vwave[t * L : (t + 1) * L, :] = block
        for source, target in ((mass_ref, mass), (pot_ref, pot)):
            block = jnp.concatenate(
                [
                    jnp.broadcast_to(source[q * tiles + t : q * tiles + t + 1, :], (cols, L))
                    for q in range(groups)
                ],
                axis=0,
            )
            target[t * L : (t + 1) * L, :] = block.T

    acc[0:L, 0:L] = jnp.zeros((L, L), F32)
    acc[0:width, 0:width] = stiff_ref[...]
    s_hi, s_lo = split(acc[0:L, 0:L])
    smat[:, 0:L] = s_hi
    smat[:, L : 2 * L] = s_lo

    cellrow[...] = jnp.full((cells, L), -1, jnp.int32)
    cellrow[:, 0:width] = map_ref[...]

    def place(n):
        g = n - nodes
        hi = jnp.where(
            g < 0,
            jnp.where(n < 0, -1, n % rows),
            rows + (g // ghost) * grows + g % grows,
        )
        q = jnp.where(g < 0, n // rows, (g // grows) % groups)
        return hi, q

    def onehot(condition):
        return jnp.where(condition, 1.0, 0.0).astype(BF)

    def tables(row, at, gather_ref, gather_at, ghosts_ref=None, ghosts_at=0):
        wide = jnp.broadcast_to(row, (L, L))
        hi_r, _ = place(wide)
        hi_c, q_c = place(wide.T)
        for t in range(gather_ref.shape[1] // L):
            gather_ref[pl.ds(gather_at, L), t * L : (t + 1) * L] = onehot(hi_c == lane + t * L)
        mask[pl.ds(at, L), :] = onehot(q_c == lane_group)
        for t in range(tiles):
            otm[t * L : (t + 1) * L, pl.ds(at, L)] = onehot(hi_r == sub + t * L)
        if ghosts_ref is not None:
            for t in range(2 * grows // L):
                ghosts_ref[t * L : (t + 1) * L, pl.ds(ghosts_at, L)] = onehot(
                    hi_r == sub + (rows + t * L)
                )

    for k, ref in enumerate((left_ref, right_ref, node_ref)):
        base = (fold0, fold0 + ghost, sup0)[k]
        for t in range(ref.shape[0]):
            tables(ref[t : t + 1, :], base + t * L, ohs, k * ghost + t * L)

    pl.semaphore_wait(
        barrier, n_col - 1 + jnp.where(outer_prev, 1, 0) + jnp.where(outer_next, 1, 0)
    )

    def halo_copy(it, side):
        return pltpu.make_async_remote_copy(
            src_ref=halo_send.at[it, side], dst_ref=halo_recv.at[it, 1 - side],
            send_sem=hs_sem.at[it, side], recv_sem=hr_sem.at[it, 1 - side],
            device_id=(prev_id, next_id)[side], device_id_type=MESH,
        )

    def back_copy(it, side):
        return pltpu.make_async_remote_copy(
            src_ref=back_send.at[it, side], dst_ref=back_recv.at[it, 1 - side],
            send_sem=bs_sem.at[it, side], recv_sem=br_sem.at[it, 1 - side],
            device_id=(prev_id, next_id)[side], device_id_type=MESH,
        )

    def proj_copy(it, k):
        return pltpu.make_async_remote_copy(
            src_ref=proj_send.at[it], dst_ref=proj_recv.at[it, k - 1],
            send_sem=ps_sem.at[it, k - 1], recv_sem=pr_sem.at[it, k - 1],
            device_id=(dom, (col + k) % n_col), device_id_type=MESH,
        )

    there = (has_prev, has_next)

    def send_halo(it):
        for t in range(tiles):
            at = slice(t * L, (t + 1) * L)
            hi, lo = split(mass[at, :] * vcur[at, :])
            field[at, 0:L] = hi
            field[at, L : 2 * L] = lo
        for side in range(2):
            packed = jnp.zeros((grows, L), F32)
            for j in range(groups):
                at = side * ghost + j * grows
                got = dot(ohs[at : at + grows, :], field[0:rows, :])
                got = (got[:, 0:L] + got[:, L:]) * mask[
                    fold0 + at : fold0 + at + grows, :
                ].astype(F32)
                packed = jnp.where(lane_group == j, replicate(got), packed)
            halo_send[it, side] = packed

            @pl.when(there[side])
            def _():
                halo_copy(it, side).start()

    def doubled(x):
        low = jnp.concatenate([x[:, 0:L], jnp.zeros((x.shape[0], L), x.dtype)], axis=1)
        return jnp.concatenate([x, low], axis=0)

    def project(it):
        got = dot(ohs[2 * ghost : 2 * ghost + slots, :], field[0:rows, :]).astype(BF)
        keep = mask[sup0 : sup0 + slots, :]
        got = got * jnp.concatenate([keep, keep], axis=1)
        part = dot(pa[...], doubled(got))
        part = replicate(part[:, 0:L] + part[:, L:])
        quarter = arows // groups
        group = lax.broadcasted_iota(jnp.int32, (quarter, L), 1) // cols
        packed = jnp.zeros((quarter, L), F32)
        for j in range(groups):
            packed = jnp.where(group == j, part[j * quarter : (j + 1) * quarter, :], packed)
        proj_send[it] = packed
        for k in range(1, n_col):
            proj_copy(it, k).start()

    def spread(it):
        for k in range(1, n_col):
            proj_copy(it, k).wait_recv()
        packed = proj_send[it]
        for k in range(1, n_col):
            packed = packed + proj_recv[it, k - 1]
        quarter = arows // groups
        group = lax.broadcasted_iota(jnp.int32, (quarter, L), 1) // cols
        for j in range(groups):
            at = slice(j * quarter, (j + 1) * quarter)
            part = replicate(jnp.where(group == j, packed, 0.0)) * cpl[at, :]
            coef[at, :] = part
        hi, lo = split(coef[...])
        back = dot(pat[...], doubled(jnp.concatenate([hi, lo], axis=1)))
        store(back[:, 0:L] + back[:, L:], sup0)

    def store(y, at):
        n = y.shape[0]
        keep = mask[pl.ds(at, n), :]
        hi, lo = split(y)
        z[pl.ds(at, n), 0:L] = hi * keep
        z[pl.ds(at, n), L : 2 * L] = lo * keep

    batch = cfg["batch"]

    def cell_step(gather_ref, first_cell, step):
        depth = gather_ref.shape[1]
        c0 = first_cell + step * batch
        local = pl.multiple_of(step * (batch * L), L)
        at = pl.multiple_of(c0 * L, L)
        got = dot(gather_ref[pl.ds(local, batch * L), :], field[0:depth, :]).astype(BF)
        keep = mask[pl.ds(at, batch * L), :]
        got = got * jnp.concatenate([keep, keep], axis=1)
        for u in range(batch):
            y = dot(smat[...], doubled(got[u * L : (u + 1) * L, :]))
            y = replicate((y[:, 0:L] + y[:, L:]) * scale_ref[c0 + u])
            store(y, pl.multiple_of(at + u * L, L))

    def cell_loop(gather_ref, first_cell, lo, hi):
        def step(s, carry):
            cell_step(gather_ref, first_cell, s)
            return carry

        lax.fori_loop(lo, hi, step, 0)

    def build_cells(lo, hi, gather_ref, ghosts_ref):
        def step(c, carry):
            local = pl.multiple_of((c - lo) * L, L)
            tables(
                cellrow[pl.ds(c, 1), :], pl.multiple_of(c * L, L), gather_ref, local,
                ghosts_ref, local,
            )
            return carry

        lax.fori_loop(lo, hi, step, 0)

    def build_atoms():
        paf[...] = jnp.zeros_like(paf)
        for t in range(slots // L):
            at = slice(t * L, (t + 1) * L)
            here = jnp.broadcast_to(atom_ref[t : t + 1, :], (nproj, L))
            values = proj_ref[:, at]
            for a in range(atoms):
                paf[a * nproj : (a + 1) * nproj, at] = jnp.where(here == a, values, 0.0)
        hi, lo = split(paf[0:arows, :])
        pa[:, 0:slots] = hi
        pa[:, slots : 2 * slots] = lo
        hi, lo = split(paf[...].T)
        pat[:, 0:apad] = hi
        pat[:, apad : 2 * apad] = lo
        for a in range(atoms):
            cpl[a * nproj : (a + 1) * nproj, :] = jnp.broadcast_to(
                coup_ref[:, a : a + 1], (nproj, L)
            )
        coef[...] = jnp.zeros_like(coef)

    send_halo(0)
    build_atoms()
    project(0)
    build_cells(0, inner, ohi, None)
    build_cells(inner, cells, ohb, otg)

    n_in = inner // batch
    n_out = (cells - inner) // batch
    early = cfg["early"]
    for it in range(2):
        if it > 0:
            send_halo(it)
            project(it)
        cell_loop(ohi, 0, 0, early)
        for side in range(2):
            @pl.when(there[side])
            def _():
                halo_copy(it, 1 - side).wait_recv()

            hi, lo = split(halo_recv[it, side])
            at = rows + side * grows
            field[at : at + grows, 0:L] = hi
            field[at : at + grows, L : 2 * L] = lo
        cell_loop(ohb, inner, 0, n_out)
        back = dot(otg[...], z[inner * L : cells * L, :])
        back = back[:, 0:L] + back[:, L:]
        for side in range(2):
            back_send[it, side] = back[side * grows : (side + 1) * grows, :]

            @pl.when(there[side])
            def _():
                back_copy(it, side).start()
        cell_loop(ohi, 0, early, n_in)
        spread(it)
        acc[...] = jnp.zeros_like(acc)
        chunk = cfg["chunk"]

        def scatter(s, carry):
            at = pl.multiple_of(s * chunk, chunk)
            acc[...] += dot(otm[:, pl.ds(at, chunk)], z[pl.ds(at, chunk), :])
            return carry

        lax.fori_loop(0, fold0 // chunk, scatter, 0)
        for side in range(2):
            @pl.when(there[side])
            def _():
                back_copy(it, 1 - side).wait_recv()

            packed = back_recv[it, side]
            for j in range(groups):
                store(
                    replicate(jnp.where(lane_group == j, packed, 0.0)),
                    fold0 + side * ghost + j * grows,
                )
        lax.fori_loop(fold0 // chunk, total // chunk, scatter, 0)
        for t in range(tiles):
            at = slice(t * L, (t + 1) * L)
            v = vcur[at, :]
            hv = mass[at, :] * (acc[at, 0:L] + acc[at, L:]) + pot[at, :] * v
            if it == 0:
                vcur[at, :] = (hv - 2.0 * v) * 0.25
            else:
                block = ((hv - 2.0 * v) * 0.5 - vwave[at, :]).T
                for q in range(groups):
                    out_ref[:, q * rows + t * L : q * rows + (t + 1) * L] = block[
                        q * cols : (q + 1) * cols, :
                    ]

    for it in range(2):
        for side in range(2):
            @pl.when(there[side])
            def _():
                halo_copy(it, side).wait_send()
                back_copy(it, side).wait_send()
        for k in range(1, n_col):
            proj_copy(it, k).wait_send()


def body(
    n_dom, n_col, wave, mass_scale, potential, stiffness, cell_scale, cell_map,
    send_left, send_right, support_node, support_atom, projector, coupling,
):
    nodes, cols = wave.shape
    ghost = send_left.shape[0]
    slots = support_node.shape[0]
    cells = cell_scale.shape[0]
    nproj, atoms = coupling.shape
    groups = L // cols
    rows = nodes // groups
    grows = ghost // groups
    inner = cells - cells // 4
    total = cells * L + slots + 2 * ghost
    arows = atoms * nproj
    apad = -(-arows // L) * L
    cfg = dict(
        n_dom=n_dom, n_col=n_col, cols=cols, groups=groups, rows=rows, cells=cells,
        inner=inner, cell_nodes=cell_map.shape[0], nodes=nodes, ghost=ghost, slots=slots,
        atoms=atoms, nproj=nproj, batch=4, early=3, chunk=512,
    )
    vm = pl.BlockSpec(memory_space=pltpu.VMEM)
    sm = pl.BlockSpec(memory_space=pltpu.SMEM)
    dma = pltpu.SemaphoreType.DMA
    out = pl.pallas_call(
        functools.partial(kernel, cfg),
        out_shape=jax.ShapeDtypeStruct((cols, nodes), F32),
        in_specs=[vm, vm, vm, vm, sm] + [vm] * 7,
        out_specs=vm,
        scratch_shapes=[
            pltpu.VMEM((rows + 2 * grows, 2 * L), BF),
            pltpu.VMEM((rows, L), F32),
            pltpu.VMEM((rows, L), F32),
            pltpu.VMEM((rows, L), F32),
            pltpu.VMEM((rows, L), F32),
            pltpu.VMEM((L, 2 * L), BF),
            pltpu.VMEM((cells, L), jnp.int32),
            pltpu.VMEM((inner * L, rows), BF),
            pltpu.VMEM(((cells - inner) * L, rows + 2 * grows), BF),
            pltpu.VMEM((2 * ghost + slots, rows), BF),
            pltpu.VMEM((rows, total), BF),
            pltpu.VMEM((2 * grows, (cells - inner) * L), BF),
            pltpu.VMEM((total, L), BF),
            pltpu.VMEM((total, 2 * L), BF),
            pltpu.VMEM((rows, 2 * L), F32),
            pltpu.VMEM((apad, slots), F32),
            pltpu.VMEM((arows, 2 * slots), BF),
            pltpu.VMEM((slots, 2 * apad), BF),
            pltpu.VMEM((arows, L), F32),
            pltpu.VMEM((apad, L), F32),
            pltpu.VMEM((2, 2, grows, L), F32),
            pltpu.VMEM((2, 2, grows, L), F32),
            pltpu.VMEM((2, 2, grows, L), F32),
            pltpu.VMEM((2, 2, grows, L), F32),
            pltpu.VMEM((2, arows // groups, L), F32),
            pltpu.VMEM((2, n_col - 1, arows // groups, L), F32),
            dma((2, 2)), dma((2, 2)), dma((2, 2)), dma((2, 2)),
            dma((2, n_col - 1)), dma((2, n_col - 1)),
        ],
        compiler_params=pltpu.CompilerParams(collective_id=0, has_side_effects=True),
        name="filter",
    )(
        wave.T, mass_scale.reshape(-1, L), potential.reshape(-1, L), stiffness, cell_scale,
        cell_map.T, send_left.reshape(-1, L), send_right.reshape(-1, L),
        support_node.reshape(-1, L), support_atom.reshape(-1, L), projector, coupling,
    )
    return out.T


def solution(mesh):
    both = ("dom", "col")
    return jax.shard_map(
        functools.partial(body, mesh.shape["dom"], mesh.shape["col"]),
        mesh=mesh,
        in_specs=(
            P(both, None), P(both), P(both), P(), P(both), P(None, both), P(both), P(both),
            P(both), P(both), P(None, both), P(None, "dom"),
        ),
        out_specs=P(both, None),
        check_vma=False,
    )
```

time: 190 us -> 43.1 us (0.23)
  other arithmetic: 73.3 us -> 0 us
  local copies, waits for them, and re-layouts: 51.2 us -> 1.67 us
  Pallas kernels: 0 us -> 41.2 us
  starting transfers between devices: 22.2 us -> 0 us
  waiting for transfers between devices: 17.9 us -> 0 us
  blocking collectives: 17.8 us -> 0 us
  matrix products: 5.84 us -> 0 us
    scatter-add x8 -> x0, other arithmetic: 69.3 us -> none  [the longest x2 46.2 us: cell_terms(): jnp.zeros((total_rows, gathered.shape[2]), jnp.float32).at[local_map]]
    pallas_call x0 -> x1, Pallas kernels: none -> 41.2 us  [body(): pl.pallas_call(functools.partial(kernel, cfg), out_shape=jax.ShapeDtypeSt...]
    gather x12 -> x0, local copies, waits for them, and re-layouts: 34.8 us -> none  [the longest x2 28.2 us: cell_terms(): gathered = field[local_map]]
    ppermute x8 -> x0, starting transfers between devices: 22.2 us -> none  [the longest x4 13.4 us: padded(): lax.ppermute(lax.slice_in_dim(block, 0, width, axis=dim), axis, backward)]
    ppermute x8 -> x0, waiting for transfers between devices: 17.9 us -> none  [the longest x4 17.9 us: padded(): lax.ppermute(lax.slice_in_dim(block, block.shape[dim] - width, None, axis...]
    psum x2 -> x0, blocking collectives: 17.8 us -> none  [apply_ham(): summed = lax.psum(partial_proj, 'col')]
    mul x4 -> x0, local copies, waits for them, and re-layouts: 6.3 us -> none  [the longest x2 5.65 us: cell_terms(): product = product.reshape(gathered.shape) * local_scale[None, :, None]]
    dot_general x6 -> x0, matrix products: 5.84 us -> none  [the longest x2 2.9 us: apply_ham(): jnp.einsum('ea,je,ajk->ek', atom_onehot, projector, coefficients, precisi...]
  transfers between devices with their start and end apart: 8 -> 0, of which waited for: 2 -> 0; matrix products, arithmetic and copies ran while one was open for 8% -> 0% of each run, Pallas kernels for 0% -> 0%
where the time goes in v1:
time: 43.1 us; the launch traced here: 42.9 us
  Pallas kernels  41.2 us (96%)
  local copies, waits for them, and re-layouts  1.67 us (4%)
    pallas_call x1, Pallas kernels, body(): pl.pallas_call(functools.partial(kernel, cfg), out_shape=jax.ShapeDtypeSt...  41.2 us
    unnamed x1, local copies, waits for them, and re-layouts  1.67 us

profile of v1, /device:TPU:1, one launch (start us, length us, event | category | flops | bytes accessed | tf_op | source)
XLA Modules:
  0.0 42.9 jit_solution(12530880589983509852)
XLA Ops:
  0.0 41.2 %filter.1 = f32[32,2048]{1,0:T(8,128)} custom-call(f32[32,2048]{1,0:T(8,128)} %bitcast.10, f32[16,128]{1,0:T(8,128)} %bitcast.12, f32[16,128]{1,0:T(8,128)} %bitcast.13, f32[125,125]{1,0:T(8,128)} %stiff_ref.1, f32[32]{0:T(128)} %scale_ref.1, s32[32,125]{1,0:T(8,128)} %bitcast.11, s32[4,128]{1,0:T(4,128)} %bitcast.14, s32[4,128]{1,0:T(4,128)} %bitcast.15, ...), custom_call_target="tpu_custom_call" | custom-call | tf_op jit(solution)/shard_map/filter/pallas_call | solution.py:403
  41.2 1.7 %copy.14 = f32[2048,32]{0,1:T(8,128)} copy(f32[2048,32]{0,1:T(8,128)} %bitcast.9) | data formatting | bytes 524288

commit v2 on v1

--- a/solution.py
+++ b/solution.py
@@ -26,12 +26,12 @@
     cfg,
     wave_ref, mass_ref, pot_ref, stiff_ref, scale_ref, map_ref,
     left_ref, right_ref, node_ref, atom_ref, proj_ref, coup_ref,
-    out_ref,
-    field, vcur, vwave, mass, pot, smat, cellrow,
+    out_hbm,
+    out_ref, field, vcur, vwave, mass, pot, smat, cellrow,
     ohi, ohb, ohs, otm, otg, mask, z, acc,
     paf, pa, pat, cpl, coef,
     halo_send, halo_recv, back_send, back_recv, proj_send, proj_recv,
-    hs_sem, hr_sem, bs_sem, br_sem, ps_sem, pr_sem,
+    out_sem, hs_sem, hr_sem, bs_sem, br_sem, ps_sem, pr_sem,
 ):
     n_dom, n_col = cfg["n_dom"], cfg["n_col"]
     cols, groups, rows = cfg["cols"], cfg["groups"], cfg["rows"]
@@ -40,6 +40,7 @@
     atoms, nproj = cfg["atoms"], cfg["nproj"]
     grows = ghost // groups
     tiles = rows // L
+    far = 2 * rows
     sup0 = cells * L
     fold0 = sup0 + slots
     total = fold0 + 2 * ghost
@@ -119,26 +120,28 @@
     smat[:, 0:L] = s_hi
     smat[:, L : 2 * L] = s_lo
 
+    def log2(x):
+        return x.bit_length() - 1
+
+    def place(n):
+        g = n - nodes
+        ghost_row = rows + ((g >> log2(ghost)) << log2(grows)) + (g & (grows - 1))
+        ghost_code = (((g >> log2(grows)) & (groups - 1)) << log2(far)) + ghost_row
+        owned_code = ((n >> log2(rows)) << log2(far)) + (n & (rows - 1))
+        return jnp.where(n < 0, far - 1, jnp.where(g < 0, owned_code, ghost_code))
+
     cellrow[...] = jnp.full((cells, L), -1, jnp.int32)
     cellrow[:, 0:width] = map_ref[...]
-
-    def place(n):
-        g = n - nodes
-        hi = jnp.where(
-            g < 0,
-            jnp.where(n < 0, -1, n % rows),
-            rows + (g // ghost) * grows + g % grows,
-        )
-        q = jnp.where(g < 0, n // rows, (g // grows) % groups)
-        return hi, q
+    cellrow[...] = place(cellrow[...])
 
     def onehot(condition):
         return jnp.where(condition, 1.0, 0.0).astype(BF)
 
     def tables(row, at, gather_ref, gather_at, ghosts_ref=None, ghosts_at=0):
         wide = jnp.broadcast_to(row, (L, L))
-        hi_r, _ = place(wide)
-        hi_c, q_c = place(wide.T)
+        hi_r = wide & (far - 1)
+        code = wide.T
+        hi_c, q_c = code & (far - 1), code >> log2(far)
         for t in range(gather_ref.shape[1] // L):
             gather_ref[pl.ds(gather_at, L), t * L : (t + 1) * L] = onehot(hi_c == lane + t * L)
         mask[pl.ds(at, L), :] = onehot(q_c == lane_group)
@@ -153,7 +156,7 @@
     for k, ref in enumerate((left_ref, right_ref, node_ref)):
         base = (fold0, fold0 + ghost, sup0)[k]
         for t in range(ref.shape[0]):
-            tables(ref[t : t + 1, :], base + t * L, ohs, k * ghost + t * L)
+            tables(place(ref[t : t + 1, :]), base + t * L, ohs, k * ghost + t * L)
 
     pl.semaphore_wait(
         barrier, n_col - 1 + jnp.where(outer_prev, 1, 0) + jnp.where(outer_next, 1, 0)
@@ -352,7 +355,7 @@
                     replicate(jnp.where(lane_group == j, packed, 0.0)),
                     fold0 + side * ghost + j * grows,
                 )
-        lax.fori_loop(fold0 // chunk, total // chunk, scatter, 0)
+        acc[...] += dot(otm[:, fold0:total], z[fold0:total, :])
         for t in range(tiles):
             at = slice(t * L, (t + 1) * L)
             v = vcur[at, :]
@@ -366,6 +369,8 @@
                         q * cols : (q + 1) * cols, :
                     ]
 
+    done = pltpu.make_async_copy(out_ref, out_hbm, out_sem)
+    done.start()
     for it in range(2):
         for side in range(2):
             @pl.when(there[side])
@@ -374,6 +379,7 @@
                 back_copy(it, side).wait_send()
         for k in range(1, n_col):
             proj_copy(it, k).wait_send()
+    done.wait()
 
 
 def body(
@@ -395,7 +401,7 @@
     cfg = dict(
         n_dom=n_dom, n_col=n_col, cols=cols, groups=groups, rows=rows, cells=cells,
         inner=inner, cell_nodes=cell_map.shape[0], nodes=nodes, ghost=ghost, slots=slots,
-        atoms=atoms, nproj=nproj, batch=4, early=3, chunk=512,
+        atoms=atoms, nproj=nproj, batch=8, early=1, chunk=1536,
     )
     vm = pl.BlockSpec(memory_space=pltpu.VMEM)
     sm = pl.BlockSpec(memory_space=pltpu.SMEM)
@@ -404,8 +410,9 @@
         functools.partial(kernel, cfg),
         out_shape=jax.ShapeDtypeStruct((cols, nodes), F32),
         in_specs=[vm, vm, vm, vm, sm] + [vm] * 7,
-        out_specs=vm,
+        out_specs=pl.BlockSpec(memory_space=pltpu.HBM),
         scratch_shapes=[
+            pltpu.VMEM((cols, nodes), F32),
             pltpu.VMEM((rows + 2 * grows, 2 * L), BF),
             pltpu.VMEM((rows, L), F32),
             pltpu.VMEM((rows, L), F32),
@@ -432,7 +439,7 @@
             pltpu.VMEM((2, 2, grows, L), F32),
             pltpu.VMEM((2, arows // groups, L), F32),
             pltpu.VMEM((2, n_col - 1, arows // groups, L), F32),
-            dma((2, 2)), dma((2, 2)), dma((2, 2)), dma((2, 2)),
+            dma(()), dma((2, 2)), dma((2, 2)), dma((2, 2)), dma((2, 2)),
             dma((2, n_col - 1)), dma((2, n_col - 1)),
         ],
         compiler_params=pltpu.CompilerParams(collective_id=0, has_side_effects=True),

time: 43.1 us -> 32.7 us (0.76)
  Pallas kernels: 41.2 us -> 30.9 us
    pallas_call x1, Pallas kernels: 41.2 us -> 30.9 us  [body(): pl.pallas_call(functools.partial(kernel, cfg), out_shape=jax.ShapeDtypeSt...]
where the time goes in v2:
time: 32.7 us; the launch traced here: 32.6 us
  Pallas kernels  30.9 us (94%)
  local copies, waits for them, and re-layouts  1.67 us (5%)
    pallas_call x1, Pallas kernels, body(): pl.pallas_call(functools.partial(kernel, cfg), out_shape=jax.ShapeDtypeSt...  30.9 us
    unnamed x1, local copies, waits for them, and re-layouts  1.67 us

profile of v2, /device:TPU:1, one launch (start us, length us, event | category | flops | bytes accessed | tf_op | source)
XLA Modules:
  0.0 32.6 jit_solution(12683186786657416356)
XLA Ops:
  0.0 30.9 %filter.1 = f32[32,2048]{1,0:T(8,128)} custom-call(f32[32,2048]{1,0:T(8,128)} %bitcast.10, f32[16,128]{1,0:T(8,128)} %bitcast.12, f32[16,128]{1,0:T(8,128)} %bitcast.13, f32[125,125]{1,0:T(8,128)} %stiff_ref.1, f32[32]{0:T(128)} %scale_ref.1, s32[32,125]{1,0:T(8,128)} %bitcast.11, s32[4,128]{1,0:T(4,128)} %bitcast.14, s32[4,128]{1,0:T(4,128)} %bitcast.15, ...), custom_call_target="tpu_custom_call" | custom-call | tf_op jit(solution)/shard_map/filter/pallas_call | solution.py:409
  30.9 1.7 %copy.14 = f32[2048,32]{0,1:T(8,128)} copy(f32[2048,32]{0,1:T(8,128)} %bitcast.9) | data formatting | bytes 524288
